TPU v7x, 256 devices: a whole 4x4x8 slice. The times are simulated.
256 devices in a mesh: row: 16 (over z, y_lo), col: 16 (over x, y_hi, core).
Axes of the slice: x: 4, y: 4 (y_hi: 2, y_lo: 2; y = y_hi * 2 + y_lo), z: 8, core: 2. Of those that a mesh axis runs over, the one named last changes fastest.
Arguments:
- raw: int32 [32768, 4096], P('col', 'row'), may hold values from -128 to 127
- taps: int32 [16, 128], replicated, may hold values from -256 to 256
Outputs:
- visibility: bfloat16 [32, 4096, 2, 4096], P(None, 'row', None, 'col')
All inputs are finite; a program needn't handle non-finite values.
Results may differ from a plain program's by a relative error of at most 0.0056.
Values may be sent and summed in bfloat16 or wider, within the bound.
A program may use at most 128 MiB of HBM per device.

v0:
```python
import math

import jax
import jax.numpy as jnp
from jax import lax
from jax.sharding import PartitionSpec as P

CHANNELS = 32
TRANSFORM = 128
TAPS = 16
SPECTRA_DEV = 16
BLOCKS = 2


def from_behind(block, axis, distance):
    devices = range(lax.axis_size(axis))
    route = [(i - distance, i) for i in devices if i - distance in devices]
    return lax.ppermute(block, axis, route)


def from_root(value, axis, root):
    mine = lax.axis_index(axis) == root
    return lax.psum(jnp.where(mine, value, jnp.zeros_like(value)), axis)


def dft_table():
    sample = jnp.arange(TRANSFORM, dtype=jnp.int32)[:, None]
    channel = jnp.arange(1, CHANNELS + 1, dtype=jnp.int32)[None, :]
    phase = (sample * channel % TRANSFORM).astype(jnp.float32) * (2.0 * math.pi / TRANSFORM)
    return jnp.concatenate([jnp.cos(phase), -jnp.sin(phase)], axis=1)


def channelize(extended, taps, count):
    coeffs = taps.astype(jnp.float32)
    weighted = jnp.zeros((count, TRANSFORM, extended.shape[2]), jnp.float32)
    for offset in range(TAPS):
        start = TAPS - 1 - offset
        weighted = weighted + coeffs[offset][None, :, None] * extended[
            start : start + count
        ].astype(jnp.float32)
    scale = 1.0 / (8192.0 * math.sqrt(TAPS * TRANSFORM))
    spectra = (
        jnp.einsum("sni,nk->ksi", weighted, dft_table(), precision=lax.Precision.HIGHEST) * scale
    )
    return spectra.reshape(2, CHANNELS, count, extended.shape[2]).astype(jnp.bfloat16)


def correlate(row_block, column_block):
    spectra_all = row_block.shape[2]
    width = spectra_all // BLOCKS
    total = None
    for block in range(BLOCKS):
        left = jnp.concatenate(
            [
                row_block[0, :, block * width : (block + 1) * width],
                row_block[1, :, block * width : (block + 1) * width],
            ],
            axis=1,
        )
        real_part = column_block[0, :, block * width : (block + 1) * width]
        imag_part = column_block[1, :, block * width : (block + 1) * width]
        right = jnp.concatenate(
            [
                jnp.concatenate([real_part, imag_part], axis=1),
                jnp.concatenate([-imag_part, real_part], axis=1),
            ],
            axis=2,
        )
        term = lax.dot_general(
            left, right, (((1,), (1,)), ((0,), (0,))), preferred_element_type=jnp.float32
        )
        if block == 0:
            total = term
        else:
            summed = total + term
            total = summed
    result = (total * (1.0 / spectra_all)).astype(jnp.bfloat16)
    return result.reshape(CHANNELS, row_block.shape[3], 2, column_block.shape[3])


def body(raw, taps):
    frames = raw.astype(jnp.bfloat16).reshape(SPECTRA_DEV, TRANSFORM, raw.shape[1])
    rim_frames = frames[SPECTRA_DEV - (TAPS - 1) :]
    earlier = from_behind(rim_frames, "col", 1)
    extended = jnp.concatenate([earlier, frames], axis=0)
    pieces = channelize(extended, taps, SPECTRA_DEV)
    row_block = lax.all_gather(pieces, "col", axis=2, tiled=True)
    ratio = lax.axis_size("row") // lax.axis_size("col")
    first_root = lax.axis_index("col") * ratio
    received = from_root(row_block, "row", first_root + 0)
    return correlate(row_block, received)


def solution(mesh):
    placed = (P("col", "row"), P())
    return jax.shard_map(
        body, mesh=mesh, in_specs=placed, out_specs=P(None, "row", None, "col"), check_vma=False
    )
```

profile of v0, /device:TPU:24, one launch (start us, length us, event | category | flops | bytes accessed | tf_op | source)
XLA Modules:
  0.0 540.1 jit_solution(9237460583808072064)
XLA Ops:
  6.5 0.0 copy-start.1
  6.5 0.0 all-gather.2.cloned.1.call-start
  6.5 1.8 convert_element_type.70
  8.3 0.1 slice.166
  8.4 1.9 collective-permute-start
  10.3 0.0 copy-done.1
  10.4 0.2 fusion.128
  10.5 14.8 %collective-permute-done = bf16[15,128,256]{2,1,0:T(8,128)(2,1)S(1)} collective-permute-done((bf16[15,128,256]{2,1,0:T(8,128)(2,1)S(1)}, bf16[15,128,256]{2,1,0:T(8,128)(2,1)S(1)}, u32[]{:S(2)}, u32[]{:S(2)}) %collective-permute-start) | collective-permute-done | bytes 983072 | tf_op jit(solution)/shard_map/ppermute | solution.py:18
  25.3 5.2 fusion.72
  30.5 1.1 copy.3
  31.6 0.0 all-gather.2.cloned.1.call-update
  31.6 0.0 all-reduce.2.cloned.1.call-start
  31.6 86.4 %all-gather.2.cloned.1.call-done = bf16[2,32,256,256]{3,2,1,0:T(8,128)(2,1)} async-done(((bf16[2,32,16,256]{3,2,1,0:T(8,128)(2,1)}), bf16[2,32,256,256]{3,2,1,0:T(8,128)(2,1)}) %all-gather.2.cloned.1.call-update) | async-done | bytes 8388624 | tf_op jit(solution)/shard_map/all_gather | solution.py:87
  118.1 3.9 broadcast_select_fusion
  122.0 0.0 all-reduce.2.cloned.1.call-update
  122.0 5.6 %slice_bitcast_fusion.3 = (bf16[32,128,256]{2,1,0:T(8,128)(2,1)S(1)}, bf16[32,128,256]{2,1,0:T(8,128)(2,1)}, bf16[32,128,256]{2,1,0:T(8,128)(2,1)}, bf16[32,128,256]{2,1,0:T(8,128)(2,1)}) fusion(bf16[2,32,256,256]{3,2,1,0:T(8,128)(2,1)} %all-gather.2.cloned.1.call-done), kind=kLoop, calls=%fused_computation.54 | loop fusion | bytes 16777216 | tf_op jit(solution)/shard_map/squeeze | solution.py:55
  127.7 362.7 %all-reduce.2.cloned.1.call-done = bf16[2,32,256,256]{3,2,1,0:T(8,128)(2,1)} async-done(((bf16[2,32,256,256]{3,2,1,0:T(8,128)(2,1)}), bf16[2,32,256,256]{3,2,1,0:T(8,128)(2,1)}) %all-reduce.2.cloned.1.call-update) | async-done | bytes 8388624 | tf_op jit(solution)/shard_map/psum | solution.py:23
  490.4 0.0 copy-start
  490.4 2.6 fusion.134
  493.0 2.0 copy-done
  495.0 3.4 slice_bitcast_fusion
  498.5 10.2 %fusion = f32[32,256,512]{2,1,0:T(8,128)} fusion(bf16[32,128,256]{2,1,0:T(8,128)(2,1)} %get-tuple-element.12, bf16[32,128,256]{2,1,0:T(8,128)(2,1)S(1)} %get-tuple-element.14, bf16[32,128,256]{2,1,0:T(8,128)(2,1)} %get-tuple-element.11, bf16[32,128,256]{2,1,0:T(8,128)(2,1)} %get-tuple-element.7, bf16[32,128,256]{2,1,0:T(8,128)(2,1)} %get-tuple-element.8), kind=kOutput, calls=%fused_computation.1 | convolution fusion | flops 2189426688 | bytes 27262976 | tf_op jit(solution)/shard_map/dot_general | solution.py:69
  508.7 12.1 %multiply_convert_fusion = bf16[32,256,512]{2,1,0:T(8,128)(2,1)} fusion(f32[32,256,512]{2,1,0:T(8,128)} %fusion, bf16[32,128,256]{2,1,0:T(8,128)(2,1)} %get-tuple-element.10, bf16[32,128,256]{2,1,0:T(8,128)(2,1)S(1)} %get-tuple-element.13, bf16[32,128,256]{2,1,0:T(8,128)(2,1)} %get-tuple-element.9, bf16[32,128,256]{2,1,0:T(8,128)(2,1)} %get-tuple-element.6, ...), kind=kOutput, calls=%fused_computation | convolution fusion | flops 2202009600 | bytes 35651584 | tf_op jit(solution)/shard_map/dot_general | solution.py:69
  520.8 12.5 %reshape.30 = bf16[32,256,2,256]{3,2,1,0:T(2,128)(2,1)} reshape(bf16[32,256,512]{2,1,0:T(8,128)(2,1)} %multiply_convert_fusion) | data formatting | bytes 16777216 | tf_op jit(solution)/shard_map/reshape | solution.py:78
  (3 shorter events, 0.0 us)
Async XLA Ops:
  6.5 3.8 copy-start.1
  6.5 111.5 %all-gather.2.cloned.1.call-start = ((), (), s32[]{:S(2)}) async-start(), calls=%async_computation | async-start | bytes 8912896 | tf_op jit(solution)/shard_map/all_gather | solution.py:87
  8.4 16.9 %collective-permute-start = (bf16[15,128,256]{2,1,0:T(8,128)(2,1)S(1)}, bf16[15,128,256]{2,1,0:T(8,128)(2,1)S(1)}, u32[]{:S(2)}, u32[]{:S(2)}) collective-permute-start(bf16[15,128,256]{2,1,0:T(8,128)(2,1)S(1)} %bitcast.59), channel_id=1, source_target_pairs={{0,1},{1,2},{2,3},{3,4},{4,5},{5,6},{6,7},{7,8},{8,9},{9,10},{10,1... | collective-permute-start | bytes 2949128 | tf_op jit(solution)/shard_map/ppermute | solution.py:18
  31.6 458.8 %all-reduce.2.cloned.1.call-start = ((), (), s32[]{:S(2)}) async-start(), calls=%async_computation.1 | async-start | bytes 16777216 | tf_op jit(solution)/shard_map/psum | solution.py:23
  490.4 4.6 copy-start
Sparse Core Ops, SparseCore 0:
  31.7 86.3 all-gather.1
  122.1 368.1 all-reduce.1
where the time goes:
time: 542 us; the launch traced here: 540 us
  waiting for transfers between devices  464 us (86%)
  matrix products  27.5 us (5%)
  local copies, waits for them, and re-layouts  24.7 us (5%)
  between operations  13.5 us (2%)
  other arithmetic  8.52 us (2%)
    psum x1, waiting for transfers between devices, from_root(): return lax.psum(jnp.where(mine, value, jnp.zeros_like(value)), axis)  363 us
    all_gather x1, waiting for transfers between devices, body(): row_block = lax.all_gather(pieces, 'col', axis=2, tiled=True)  86.4 us
    dot_general x2, matrix products, correlate(): lax.dot_general(left, right, (((1,), (1,)), ((0,), (0,))), preferred_elem...  22.3 us
    ppermute x1, waiting for transfers between devices, from_behind(): return lax.ppermute(block, axis, route)  14.8 us
    reshape x1, local copies, waits for them, and re-layouts, correlate(): result.reshape(CHANNELS, row_block.shape[3], 2, column_block.shape[3])  12.5 us
  transfers between devices with their start and end apart: 3, of which 3 were waited for; matrix products, arithmetic and copies ran while one was open for 1% of the time, Pallas kernels for 0%

commit v1 on v0

--- a/solution.py
+++ b/solution.py
@@ -18,9 +18,10 @@
     return lax.ppermute(block, axis, route)
 
 
-def from_root(value, axis, root):
-    mine = lax.axis_index(axis) == root
-    return lax.psum(jnp.where(mine, value, jnp.zeros_like(value)), axis)
+def swap_block(block):
+    size = lax.axis_size("row")
+    route = [(i * size + j, j * size + i) for i in range(size) for j in range(size)]
+    return lax.ppermute(block, ("row", "col"), route)
 
 
 def dft_table():
@@ -84,11 +85,10 @@
     earlier = from_behind(rim_frames, "col", 1)
     extended = jnp.concatenate([earlier, frames], axis=0)
     pieces = channelize(extended, taps, SPECTRA_DEV)
+    swapped = swap_block(pieces)
     row_block = lax.all_gather(pieces, "col", axis=2, tiled=True)
-    ratio = lax.axis_size("row") // lax.axis_size("col")
-    first_root = lax.axis_index("col") * ratio
-    received = from_root(row_block, "row", first_root + 0)
-    return correlate(row_block, received)
+    column_block = lax.all_gather(swapped, "row", axis=2, tiled=True)
+    return correlate(row_block, column_block)
 
 
 def solution(mesh):

time: 542 us -> 381 us (0.70)
  waiting for transfers between devices: 464 us -> 283 us
  local copies, waits for them, and re-layouts: 24.7 us -> 43.6 us
    psum x1 -> x0, waiting for transfers between devices: 363 us -> none  [from_root(): return lax.psum(jnp.where(mine, value, jnp.zeros_like(value)), axis)]
    all_gather x0 -> x1, waiting for transfers between devices: none -> 161 us  [body(): column_block = lax.all_gather(swapped, 'row', axis=2, tiled=True)]
    ppermute x0 -> x1, waiting for transfers between devices: none -> 34.3 us  [swap_block(): return lax.ppermute(block, ('row', 'col'), route)]
    unnamed x4 -> x16, local copies, waits for them, and re-layouts: 2 us -> 19.7 us
    all_gather x1, waiting for transfers between devices: 86.4 us -> 73 us  [body(): row_block = lax.all_gather(pieces, 'col', axis=2, tiled=True)]
    slice x0 -> x1, local copies, waits for them, and re-layouts: none -> 5.8 us  [correlate(): row_block[0, :, block * width:(block + 1) * width]]
    squeeze x1 -> x0, local copies, waits for them, and re-layouts: 5.65 us -> none  [correlate(): row_block[0, :, block * width:(block + 1) * width]]
  transfers between devices with their start and end apart: 3 -> 4, of which waited for: 3 -> 4; matrix products, arithmetic and copies ran while one was open for 1% -> 6% of each run, Pallas kernels for 0% -> 0%
where the time goes in v1:
time: 381 us; the launch traced here: 379 us
  waiting for transfers between devices  283 us (74%)
  local copies, waits for them, and re-layouts  43.6 us (11%)
  matrix products  28.9 us (8%)
  between operations  13.5 us (4%)
  other arithmetic  5.91 us (2%)
  starting transfers between devices  4.38 us (1%)
    all_gather x1, waiting for transfers between devices, body(): column_block = lax.all_gather(swapped, 'row', axis=2, tiled=True)  161 us
    all_gather x1, waiting for transfers between devices, body(): row_block = lax.all_gather(pieces, 'col', axis=2, tiled=True)  73 us
    ppermute x1, waiting for transfers between devices, swap_block(): return lax.ppermute(block, ('row', 'col'), route)  34.3 us
    dot_general x2, matrix products, correlate(): lax.dot_general(left, right, (((1,), (1,)), ((0,), (0,))), preferred_elem...  22.9 us
    unnamed x16, local copies, waits for them, and re-layouts  19.7 us
    ppermute x1, waiting for transfers between devices, from_behind(): return lax.ppermute(block, axis, route)  14.8 us
    reshape x1, local copies, waits for them, and re-layouts, correlate(): result.reshape(CHANNELS, row_block.shape[3], 2, column_block.shape[3])  12.5 us
  transfers between devices with their start and end apart: 4, of which 4 were waited for; matrix products, arithmetic and copies ran while one was open for 6% of the time, Pallas kernels for 0%

profile of v1, /device:TPU:24, one launch (start us, length us, event | category | flops | bytes accessed | tf_op | source)
XLA Modules:
  0.0 379.0 jit_solution(359038543877682941)
XLA Ops:
  6.5 0.0 copy-start.5
  6.5 0.0 all-gather.3.cloned.1.call-start
  6.5 1.8 convert_element_type.70
  8.3 0.1 slice.166
  8.4 1.9 collective-permute-start
  10.3 0.0 copy-done.5
  10.4 0.2 fusion.128
  10.5 14.8 %collective-permute-done = bf16[15,128,256]{2,1,0:T(8,128)(2,1)S(1)} collective-permute-done((bf16[15,128,256]{2,1,0:T(8,128)(2,1)S(1)}, bf16[15,128,256]{2,1,0:T(8,128)(2,1)S(1)}, u32[]{:S(2)}, u32[]{:S(2)}) %collective-permute-start) | collective-permute-done | bytes 983072 | tf_op jit(solution)/shard_map/ppermute | solution.py:18
  25.3 6.0 %fusion.72 = bf16[64,16,256]{2,0,1:T(8,128)(2,1)} fusion(bf16[16,128,256]{2,1,0:T(8,128)(2,1)S(1)} %bitcast.54, bf16[15,128,256]{2,1,0:T(8,128)(2,1)S(1)} %collective-permute-done, f32[128]{0:T(128)S(1)} %get-tuple-element.16, f32[128]{0:T(128)S(1)} %get-tuple-element.17, f32[128]{0:T(128)S(1)} %get-tuple-element.18, f32[128]{0:T(128)S(1)} %get-tuple-element.19, ...), kind=kOutput, calls=%fused_computation.103 | convolution fusion | flops 451420160 | bytes 2596864 | tf_op jit(solution)/shard_map/sni,nk->ksi/dot_general | solution.py:44
  31.3 0.0 all-gather.3.cloned.1.call-update
  31.3 0.0 all-gather.5.cloned.1.call-start
  31.3 1.3 copy.7
  32.7 2.4 collective-permute-start.1
  35.1 34.3 %collective-permute-done.1 = bf16[2,32,16,256]{3,2,1,0:T(8,128)(2,1)S(1)} collective-permute-done((bf16[2,32,16,256]{3,2,1,0:T(8,128)(2,1)S(1)}, bf16[2,32,16,256]{3,2,1,0:T(8,128)(2,1)S(1)}, u32[]{:S(2)}, u32[]{:S(2)}) %collective-permute-start.1) | collective-permute-done | bytes 524320 | tf_op jit(solution)/shard_map/ppermute | solution.py:24
  69.4 0.8 copy-done.4
  70.2 0.0 all-gather.5.cloned.1.call-update
  70.2 73.0 %all-gather.3.cloned.1.call-done = bf16[2,32,256,256]{3,1,0,2:T(8,128)(2,1)} async-done(((bf16[2,32,16,256]{3,1,0,2:T(8,128)(2,1)}), bf16[2,32,256,256]{3,1,0,2:T(8,128)(2,1)}) %all-gather.3.cloned.1.call-update) | async-done | bytes 8388624 | tf_op jit(solution)/shard_map/all_gather | solution.py:89
  143.2 5.8 %fusion.135 = (bf16[1,32,128,256]{3,1,0,2:T(8,128)(2,1)}, bf16[1,32,128,256]{3,1,0,2:T(8,128)(2,1)}, bf16[1,32,128,256]{3,1,0,2:T(8,128)(2,1)}, bf16[1,32,128,256]{3,1,0,2:T(8,128)(2,1)S(1)}) fusion(bf16[2,32,256,256]{3,1,0,2:T(8,128)(2,1)} %all-gather.3.cloned.1.call-done), kind=kLoop, calls=%fused_computation.173 | loop fusion | bytes 16777216 | tf_op jit(solution)/shard_map/slice | solution.py:56
  149.0 4.5 %copy.12 = bf16[1,32,128,256]{2,3,1,0:T(8,128)(2,1)} copy(bf16[1,32,128,256]{3,1,0,2:T(8,128)(2,1)} %get-tuple-element.5) | data formatting | bytes 4194304
  153.5 4.5 %copy.11 = bf16[1,32,128,256]{2,3,1,0:T(8,128)(2,1)} copy(bf16[1,32,128,256]{3,1,0,2:T(8,128)(2,1)} %get-tuple-element.6) | data formatting | bytes 4194304
  158.1 4.5 %copy.10 = bf16[1,32,128,256]{2,3,1,0:T(8,128)(2,1)} copy(bf16[1,32,128,256]{3,1,0,2:T(8,128)(2,1)} %get-tuple-element.7) | data formatting | bytes 4194304
  162.6 3.1 copy.13
  165.7 160.7 %all-gather.5.cloned.1.call-done = bf16[2,32,256,256]{3,2,1,0:T(8,128)(2,1)} async-done(((bf16[2,32,16,256]{3,2,1,0:T(8,128)(2,1)}), bf16[2,32,256,256]{3,2,1,0:T(8,128)(2,1)}) %all-gather.5.cloned.1.call-update) | async-done | bytes 8388624 | tf_op jit(solution)/shard_map/all_gather | solution.py:90
  326.4 4.0 %fusion.134 = (bf16[32,128,256]{2,1,0:T(8,128)(2,1)}, bf16[32,128,256]{2,1,0:T(8,128)(2,1)S(1)}) fusion(bf16[2,32,256,256]{3,2,1,0:T(8,128)(2,1)} %all-gather.5.cloned.1.call-done), kind=kLoop, calls=%fused_computation.172 | loop fusion | flops 2097152 | bytes 8388608 | tf_op jit(solution)/shard_map/neg | solution.py:66
  330.4 1.4 copy-done
  331.8 4.2 %slice_bitcast_fusion = (bf16[32,128,256]{2,1,0:T(8,128)(2,1)}, bf16[32,128,256]{2,1,0:T(8,128)(2,1)}, bf16[32,128,256]{2,1,0:T(8,128)(2,1)}, bf16[32,128,256]{2,1,0:T(8,128)(2,1)}) fusion(bf16[2,32,256,256]{3,2,1,0:T(8,128)(2,1)S(1)} %copy-done), kind=kLoop, calls=%fused_computation.50 | loop fusion | bytes 16777216 | tf_op jit(solution)/shard_map/squeeze | solution.py:62
  336.0 0.0 copy-done.2
  336.0 0.8 copy-done.3
  336.8 9.2 %fusion = f32[32,256,512]{2,1,0:T(8,128)} fusion(bf16[32,128,256]{2,1,0:T(8,128)(2,1)} %get-tuple-element.12, bf16[32,128,256]{2,1,0:T(8,128)(2,1)S(1)} %get-tuple-element.14, bf16[32,128,256]{2,1,0:T(8,128)(2,1)} %get-tuple-element.11, bf16[32,128,256]{1,2,0:T(8,128)(2,1)S(1)} %bitcast.57, bf16[32,128,256]{1,2,0:T(8,128)(2,1)S(1)} %bitcast.58), kind=kOutput, calls=%fused_computation.1 | convolution fusion | flops 2189426688 | bytes 27262976 | tf_op jit(solution)/shard_map/dot_general | solution.py:70
  346.1 0.0 copy-done.1
  346.1 13.7 %multiply_convert_fusion = bf16[32,256,512]{2,1,0:T(8,128)(2,1)} fusion(f32[32,256,512]{2,1,0:T(8,128)} %fusion, bf16[32,128,256]{2,1,0:T(8,128)(2,1)} %get-tuple-element.10, bf16[32,128,256]{2,1,0:T(8,128)(2,1)} %get-tuple-element.13, bf16[32,128,256]{2,1,0:T(8,128)(2,1)} %get-tuple-element.9, bf16[32,128,256]{1,2,0:T(8,128)(2,1)} %bitcast.56, ...), kind=kOutput, calls=%fused_computation | convolution fusion | flops 2202009600 | bytes 35651584 | tf_op jit(solution)/shard_map/dot_general | solution.py:70
  359.7 12.5 %reshape.30 = bf16[32,256,2,256]{3,2,1,0:T(2,128)(2,1)} reshape(bf16[32,256,512]{2,1,0:T(8,128)(2,1)} %multiply_convert_fusion) | data formatting | bytes 16777216 | tf_op jit(solution)/shard_map/reshape | solution.py:79
  (8 shorter events, 0.0 us)
Async XLA Ops:
  6.5 3.8 copy-start.5
  6.5 136.7 %all-gather.3.cloned.1.call-start = ((), (), s32[]{:S(2)}) async-start(), calls=%async_computation | async-start | bytes 8912896 | tf_op jit(solution)/shard_map/all_gather | solution.py:89
  8.4 16.9 %collective-permute-start = (bf16[15,128,256]{2,1,0:T(8,128)(2,1)S(1)}, bf16[15,128,256]{2,1,0:T(8,128)(2,1)S(1)}, u32[]{:S(2)}, u32[]{:S(2)}) collective-permute-start(bf16[15,128,256]{2,1,0:T(8,128)(2,1)S(1)} %bitcast.61), channel_id=1, source_target_pairs={{0,1},{1,2},{2,3},{3,4},{4,5},{5,6},{6,7},{7,8},{8,9},{9,10},{10,1... | collective-permute-start | bytes 2949128 | tf_op jit(solution)/shard_map/ppermute | solution.py:18
  31.3 295.1 %all-gather.5.cloned.1.call-start = ((), (), s32[]{:S(2)}) async-start(), calls=%async_computation.1 | async-start | bytes 8912896 | tf_op jit(solution)/shard_map/all_gather | solution.py:90
  32.7 36.7 %collective-permute-start.1 = (bf16[2,32,16,256]{3,2,1,0:T(8,128)(2,1)S(1)}, bf16[2,32,16,256]{3,2,1,0:T(8,128)(2,1)S(1)}, u32[]{:S(2)}, u32[]{:S(2)}) collective-permute-start(bf16[2,32,16,256]{3,2,1,0:T(8,128)(2,1)S(1)} %copy.7), channel_id=1, source_target_pairs={{0,0},{1,16},{2,32},{3,48},{4,64},{5,80},{6,96},{7,112},{8,128},{9... | collective-permute-start | bytes 1572872 | tf_op jit(solution)/shard_map/ppermute | solution.py:24
  69.4 0.8 copy-start.4
  326.4 5.4 %copy-start = (bf16[2,32,256,256]{3,2,1,0:T(8,128)(2,1)S(1)}, bf16[2,32,256,256]{3,2,1,0:T(8,128)(2,1)}, u32[]{:S(2)}) copy-start(bf16[2,32,256,256]{3,2,1,0:T(8,128)(2,1)} %all-gather.5.cloned.1.call-done) | copy-start | bytes 25165828
  331.8 4.2 %copy-start.2 = (bf16[1,32,128,256]{2,3,1,0:T(8,128)(2,1)S(1)}, bf16[1,32,128,256]{2,3,1,0:T(8,128)(2,1)}, u32[]{:S(2)}) copy-start(bf16[1,32,128,256]{2,3,1,0:T(8,128)(2,1)} %copy.11) | copy-start | bytes 6291460
  331.8 5.0 %copy-start.3 = (bf16[1,32,128,256]{2,3,1,0:T(8,128)(2,1)S(1)}, bf16[1,32,128,256]{2,3,1,0:T(8,128)(2,1)}, u32[]{:S(2)}) copy-start(bf16[1,32,128,256]{2,3,1,0:T(8,128)(2,1)} %copy.10) | copy-start | bytes 6291460
  336.8 9.2 %copy-start.1 = (bf16[1,32,128,256]{2,3,1,0:T(8,128)(2,1)S(1)}, bf16[1,32,128,256]{2,3,1,0:T(8,128)(2,1)}, u32[]{:S(2)}) copy-start(bf16[1,32,128,256]{2,3,1,0:T(8,128)(2,1)} %copy.12) | copy-start | bytes 6291460
Sparse Core Ops, SparseCore 0:
  31.4 111.7 all-gather.2
  145.0 181.3 all-gather.4

commit v2 on v1

v2 whole, which is shorter than its diff:
```python
import math

import jax
import jax.numpy as jnp
import ml_dtypes
import numpy as np
from jax import lax
from jax.experimental import pallas as pl
from jax.experimental.pallas import tpu as pltpu
from jax.sharding import PartitionSpec as P

CHANNELS = 32
TRANSFORM = 128
TAPS = 16
SPECTRA_DEV = 16
SPECTRA = 256
UNITS = 2 * CHANNELS
SIDE = 256
LAG = 8
SPLIT = 2
GROUP = 2
GROUPS = UNITS // GROUP
LEAD = 4
END = 8 * LAG // 2
RIM = TAPS - 1
STRIPS = [(11, 15), (7, 11), (3, 7), (0, 3)]
MESH = pl.DeviceIdType.MESH


def dft_tables():
    sample = np.arange(TRANSFORM)[None, :]
    channel = np.arange(1, CHANNELS + 1)[:, None]
    phase = (sample * channel % TRANSFORM) * (2.0 * math.pi / TRANSFORM)
    rest = np.stack([np.cos(phase), -np.sin(phase)], axis=1).reshape(UNITS, TRANSFORM)
    rest = rest.astype(np.float32)
    parts = []
    for _ in range(3):
        part = rest.astype(ml_dtypes.bfloat16)
        rest = rest - part.astype(np.float32)
        parts.append(part)
    one, two, three = parts
    first = np.block([[one, one], [three, two]])
    second = np.block([[two, one]])
    return np.concatenate([first, second], axis=0)


def product(a, b):
    return lax.dot_general(a, b, (((0,), (0,)), ((), ())), preferred_element_type=jnp.float32)


def own_filter(raw_ref, taps_ref, acc):
    def tile(i, carry):
        rows = pl.multiple_of(i * 8, 8)
        for half in range(2):
            lanes = pl.ds(half * 128, 128)
            taps = [taps_ref[p, pl.ds(rows, 8), :] for p in range(TAPS)]
            frames = [
                raw_ref[pl.ds(s * TRANSFORM + rows, 8), lanes].astype(jnp.float32)
                for s in range(SPECTRA_DEV)
            ]
            for s in range(SPECTRA_DEV):
                total = taps[0] * frames[s]
                for p in range(1, s + 1):
                    total = total + taps[p] * frames[s - p]
                acc[s, pl.ds(rows, 8), lanes] = total
        return carry

    lax.fori_loop(0, TRANSFORM // 8, tile, 0)


def rim_filter(low, high, rim, taps_ref, acc):
    def tile(i, carry):
        rows = pl.multiple_of(i * 16, 16)
        for half in range(2):
            lanes = pl.ds(half * 128, 128)
            frames = [
                rim[j, pl.ds(rows, 16), lanes].astype(jnp.float32) for j in range(low, high)
            ]
            for s in range(high):
                total = acc[s, pl.ds(rows, 16), lanes]
                for j in range(max(s, low), high):
                    tap = taps_ref[RIM + s - j, pl.ds(rows, 16), :]
                    total = total + tap * frames[j - low]
                acc[s, pl.ds(rows, 16), lanes] = total
        return carry

    lax.fori_loop(0, TRANSFORM // 16, tile, 0)


def spread_taps(table_ref, spread):
    taps = table_ref[3 * UNITS :, :TRANSFORM]
    index = lax.broadcasted_iota(jnp.int32, (TAPS, 128), 0)
    for p in range(TAPS):
        pick = jnp.where(index == p, 1.0, 0.0).astype(jnp.bfloat16)
        spread[p] = product(taps, pick)


def transform(low, high, table_ref, acc, flat):
    scale = 1.0 / (8192.0 * math.sqrt(TAPS * TRANSFORM))

    def one(s, carry):
        value = acc[s]
        high = value.astype(jnp.bfloat16)
        rest = value - high.astype(jnp.float32)
        mid = rest.astype(jnp.bfloat16)
        low = (rest - mid.astype(jnp.float32)).astype(jnp.bfloat16)
        most = jnp.dot(
            table_ref[: 2 * UNITS, :], jnp.concatenate([high, mid], axis=0),
            preferred_element_type=jnp.float32,
        )
        less = jnp.dot(
            table_ref[2 * UNITS : 3 * UNITS, :], jnp.concatenate([high, low], axis=0),
            preferred_element_type=jnp.float32,
        )
        result = (most[:UNITS] + (less + most[UNITS:])) * scale
        rows = pl.ds(pl.multiple_of(s * UNITS, UNITS), UNITS)
        for half in range(2):
            flat[half, rows, :] = result[:, half * 128 : (half + 1) * 128]
        return carry

    lax.fori_loop(low, high, one, 0)


def gather_correlate(
    raw_ref, table_ref, o_ref, a, b, rim, own_rim, acc, flat, taps_ref, rim_sem, y_sem, x_sem,
    s_sem, z_sem, f_sem, out_sem,
):
    r = lax.axis_index("row")
    c = lax.axis_index("col")
    z, yl = r // 2, r % 2
    x, yh, co = c // 4, (c // 2) % 2, c % 2
    flip_r = r + 1 - 2 * yl
    at_x = 2 * x
    place = at_x + yh
    rest = pl.ds(0, SPLIT)
    far = pl.ds(SPLIT, 8 - SPLIT)
    flip_y = c + 2 - 4 * yh
    flip_core = c + 1 - 2 * co
    z_next = [((r + 2) % 16, c), ((r + 14) % 16, c)]
    x_next = [(r, (c + 4 * d) % 16) for d in (1, 2, 3)]
    pair = (flip_r, c)
    cross = (flip_r, flip_y)
    sibling = (r, flip_core)
    across = (r, flip_y)

    barrier = pltpu.get_barrier_semaphore()
    after = (r, (c + 1) % 16)
    before = (r, (c + 15) % 16)
    for peer in z_next + x_next + [pair, cross, sibling, across, after, before]:
        pl.semaphore_signal(barrier, inc=1, device_id=peer, device_id_type=MESH)
    spread_taps(table_ref, taps_ref)
    for s in range(RIM):
        own_rim[s] = raw_ref[(s + 1) * TRANSFORM : (s + 2) * TRANSFORM, :].astype(jnp.bfloat16)
    pl.semaphore_wait(barrier, 11)

    dz = (z - c // 2 + 8) % 8
    main = yl == co
    root = jnp.logical_and(main, dz == 0)
    helper = r == flip_y
    hops = dz + jnp.where(main, 0, 1)
    back = (8 - dz) % 8 + jnp.where(main, 0, 1)
    begin = [LAG * hops // 2, LAG * back // 2]
    more = [dz != 7, dz != 1]

    def remote(src, dst, send, recv, peer):
        return pltpu.make_async_remote_copy(
            src_ref=src, dst_ref=dst, send_sem=send, recv_sem=recv, device_id=peer,
            device_id_type=MESH,
        )

    def arrived(dst, sem):
        remote(dst, dst, sem, sem, pair).wait_recv()

    def strip_copy(q):
        frames = pl.ds(STRIPS[q][0], STRIPS[q][1] - STRIPS[q][0])
        return remote(
            own_rim.at[frames], rim.at[frames], out_sem.at[11], rim_sem.at[q], after
        )

    @pl.when(c < 15)
    def _():
        for q in range(len(STRIPS)):
            strip_copy(q).start()

    @pl.when(c == 0)
    def _():
        rim[...] = jnp.zeros_like(rim)

    own_filter(raw_ref, taps_ref, acc)
    done = SPECTRA_DEV
    for q, (low, high) in enumerate(STRIPS):
        @pl.when(c > 0)
        def _():
            strip_copy(q).wait_recv()

        rim_filter(low, high, rim, taps_ref, acc)
        transform(low, done, table_ref, acc, flat)
        done = low

    def send_across(j, carry):
        for e in range(GROUP):
            u = j * GROUP + e
            for half in range(2):
                lanes = pl.ds(half * 128, 128)
                rows = flat[half, pl.ds(u, SPECTRA_DEV, stride=UNITS), :]
                a[u, co, place, :, lanes] = rows.astype(jnp.bfloat16)
        rows = pl.ds(j * GROUP, GROUP)
        remote(
            a.at[rows, co, place], a.at[rows, co, place], out_sem.at[0], y_sem.at[j], across
        ).start()
        return carry

    lax.fori_loop(0, GROUPS, send_across, 0)

    def step(i, carry):
        t = i - 2 * LEAD

        @pl.when(jnp.logical_and(t % GROUP == 0, t < UNITS))
        def _():
            j = t // GROUP

            @pl.when(t >= 0)
            def _():
                arrived(a.at[pl.ds(j * GROUP, GROUP), 1 - co], s_sem.at[j])

            m = j + 2 * LEAD // GROUP

            @pl.when(m < GROUPS)
            def _():
                rows = pl.ds(m * GROUP, GROUP)
                arrived(a.at[rows, co, at_x + 1 - yh], y_sem.at[m])
                for d in range(3):
                    remote(
                        a.at[rows, co, pl.ds(at_x, 2)], a.at[rows, co, pl.ds(at_x, 2)], out_sem.at[1 + d],
                        x_sem.at[d, m], x_next[d],
                    ).start()

            n = j + LEAD // GROUP

            @pl.when(jnp.logical_and(n >= 0, n < GROUPS))
            def _():
                rows = pl.ds(n * GROUP, GROUP)
                for d in range(3):
                    arrived(a.at[rows, co, pl.ds((x + 3 - d) % 4 * 2, 2)], x_sem.at[d, n])
                remote(
                    a.at[rows, co], a.at[rows, co], out_sem.at[4], s_sem.at[n], sibling
                ).start()

        for h in range(2):
            u = t - begin[h]

            @pl.when(jnp.logical_and(u >= 0, u < UNITS))
            def _():
                @pl.when(root)
                def _():
                    remote(
                        a.at[u, h], b.at[u, h], out_sem.at[5 + h], z_sem.at[h, u], z_next[h]
                    ).start()
                    remote(
                        a.at[u, h, rest], b.at[u, h, rest], out_sem.at[7 + h], z_sem.at[h, u], pair
                    ).start()
                    pltpu.make_async_copy(a.at[u, h], b.at[u, h], f_sem.at[h, u]).start()

                @pl.when(jnp.logical_and(main, jnp.logical_not(root)))
                def _():
                    arrived(b.at[u, h], z_sem.at[h, u])

                    @pl.when(more[h])
                    def _():
                        remote(
                            b.at[u, h], b.at[u, h], out_sem.at[5 + h], z_sem.at[h, u], z_next[h]
                        ).start()

                    remote(
                        b.at[u, h, far], b.at[u, h, far], out_sem.at[7 + h], f_sem.at[h, u], pair
                    ).start()

                @pl.when(jnp.logical_not(main))
                def _():
                    arrived(b.at[u, h, rest], z_sem.at[h, u])

                    @pl.when(more[h])
                    def _():
                        remote(
                            b.at[u, h, rest], b.at[u, h, rest], out_sem.at[5 + h], z_sem.at[h, u],
                            z_next[h],
                        ).start()

        @pl.when(jnp.logical_and(helper, jnp.logical_and(t >= 0, t < UNITS)))
        def _():
            for h in range(2):
                remote(
                    a.at[t, h, far], b.at[t, h, far], out_sem.at[9 + h], f_sem.at[h, t], cross
                ).start()

        v = t - END - 1

        @pl.when(jnp.logical_and(v >= 0, v % 2 == 0))
        def _():
            for e in range(2):
                for h in range(2):
                    @pl.when(root)
                    def _():
                        pltpu.make_async_copy(
                            a.at[v + e, h], b.at[v + e, h], f_sem.at[h, v + e]
                        ).wait()

                    @pl.when(jnp.logical_not(main))
                    def _():
                        arrived(b.at[v + e, h, far], f_sem.at[h, v + e])

            a_re = a[v].reshape(SIDE, SIDE)
            a_im = a[v + 1].reshape(SIDE, SIDE)
            b_re = b[v].reshape(SIDE, SIDE)
            b_im = b[v + 1].reshape(SIDE, SIDE)
            real = product(a_re, b_re) + product(a_im, b_im)
            imag = product(a_im, b_re) - product(a_re, b_im)
            k = v // 2
            o_ref[k, :, 0, :] = (real * (1.0 / SPECTRA)).astype(jnp.bfloat16)
            o_ref[k, :, 1, :] = (imag * (1.0 / SPECTRA)).astype(jnp.bfloat16)

        return carry

    lax.fori_loop(0, UNITS + END + 2 * LEAD, step, 0)

    def left(src, sem):
        remote(src, src, sem, sem, pair).wait_send()

    @pl.when(c < 15)
    def _():
        left(own_rim, out_sem.at[11])

    left(a.at[:, co, place], out_sem.at[0])
    for d in range(3):
        left(a.at[:, co, pl.ds(at_x, 2)], out_sem.at[1 + d])
    left(a.at[:, co], out_sem.at[4])
    for h in range(2):
        @pl.when(jnp.logical_and(main, more[h]))
        def _():
            left(b.at[:, h], out_sem.at[5 + h])

        @pl.when(jnp.logical_and(jnp.logical_not(main), more[h]))
        def _():
            left(b.at[:, h, rest], out_sem.at[5 + h])

        @pl.when(root)
        def _():
            left(b.at[:, h, rest], out_sem.at[7 + h])

        @pl.when(jnp.logical_and(main, jnp.logical_not(root)))
        def _():
            left(b.at[:, h, far], out_sem.at[7 + h])

        @pl.when(helper)
        def _():
            left(a.at[:, h, far], out_sem.at[9 + h])


def body(raw, taps):
    wide = jnp.concatenate([taps, jnp.zeros_like(taps)], axis=1).astype(jnp.bfloat16)
    table = jnp.concatenate([dft_tables(), wide], axis=0)
    block = (UNITS, 2, 8, SPECTRA_DEV, SIDE)
    dma = pltpu.SemaphoreType.DMA
    return pl.pallas_call(
        gather_correlate,
        out_shape=jax.ShapeDtypeStruct((CHANNELS, SIDE, 2, SIDE), jnp.bfloat16),
        in_specs=[pl.BlockSpec(memory_space=pltpu.VMEM)] * 2,
        out_specs=pl.BlockSpec(memory_space=pltpu.VMEM),
        scratch_shapes=[
            pltpu.VMEM(block, jnp.bfloat16),
            pltpu.VMEM(block, jnp.bfloat16),
            pltpu.VMEM((RIM, TRANSFORM, SIDE), jnp.bfloat16),
            pltpu.VMEM((RIM, TRANSFORM, SIDE), jnp.bfloat16),
            pltpu.VMEM((SPECTRA_DEV, TRANSFORM, SIDE), jnp.float32),
            pltpu.VMEM((2, SPECTRA_DEV * UNITS, 128), jnp.float32),
            pltpu.VMEM((TAPS, TRANSFORM, 128), jnp.float32),
            dma((len(STRIPS),)),
            dma((GROUPS,)),
            dma((3, GROUPS)),
            dma((GROUPS,)),
            dma((2, UNITS)),
            dma((2, UNITS)),
            dma((12,)),
        ],
        compiler_params=pltpu.CompilerParams(
            collective_id=0, has_side_effects=True, vmem_limit_bytes=30 * 1024 * 1024
        ),
    )(raw, table)


def solution(mesh):
    placed = (P("col", "row"), P())
    return jax.shard_map(
        body, mesh=mesh, in_specs=placed, out_specs=P(None, "row", None, "col"), check_vma=False
    )
```

time: 381 us -> 132 us (0.35)
  waiting for transfers between devices: 283 us -> 0 us
  Pallas kernels: 0 us -> 125 us
  local copies, waits for them, and re-layouts: 43.6 us -> 4.99 us
  matrix products: 28.9 us -> 0 us
  between operations: 13.5 us -> 0.02 us
  starting transfers between devices: 4.38 us -> 0 us
  other arithmetic: 5.91 us -> 1.6 us
    all_gather x2 -> x0, waiting for transfers between devices: 234 us -> none  [the longest x1 161 us: body(): column_block = lax.all_gather(swapped, 'row', axis=2, tiled=True)]
    pallas_call x0 -> x1, Pallas kernels: none -> 125 us  [body(): pl.pallas_call(gather_correlate, out_shape=jax.ShapeDtypeStruct((CHANNELS...]
    ppermute x2 -> x0, waiting for transfers between devices: 49.1 us -> none  [the longest x1 34.3 us: swap_block(): return lax.ppermute(block, ('row', 'col'), route)]
    dot_general x3 -> x0, matrix products: 28.9 us -> none  [the longest x2 22.9 us: correlate(): lax.dot_general(left, right, (((1,), (1,)), ((0,), (0,))), preferred_elem...]
    unnamed x16 -> x3, local copies, waits for them, and re-layouts: 19.7 us -> 4.99 us
    reshape x1 -> x0, local copies, waits for them, and re-layouts: 12.5 us -> none  [correlate(): result.reshape(CHANNELS, row_block.shape[3], 2, column_block.shape[3])]
    slice x2 -> x0, local copies, waits for them, and re-layouts: 5.87 us -> none  [the longest x1 5.8 us: correlate(): row_block[0, :, block * width:(block + 1) * width]]
    ppermute x2 -> x0, starting transfers between devices: 4.33 us -> none  [the longest x1 2.41 us: swap_block(): return lax.ppermute(block, ('row', 'col'), route)]
  transfers between devices with their start and end apart: 4 -> 0, of which waited for: 4 -> 0; matrix products, arithmetic and copies ran while one was open for 6% -> 0% of each run, Pallas kernels for 0% -> 0%
where the time goes in v2:
time: 132 us; the launch traced here: 131 us
  Pallas kernels  125 us (95%)
  local copies, waits for them, and re-layouts  4.99 us (4%)
  other arithmetic  1.6 us (1%)
    pallas_call x1, Pallas kernels, body(): pl.pallas_call(gather_correlate, out_shape=jax.ShapeDtypeStruct((CHANNELS...  125 us
    unnamed x3, local copies, waits for them, and re-layouts  4.99 us

profile of v2, /device:TPU:24, one launch (start us, length us, event | category | flops | bytes accessed | tf_op | source)
XLA Modules:
  0.0 131.5 jit_solution(14010305010056622791)
XLA Ops:
  0.0 0.7 convert.4
  0.7 0.9 fusion.1.table_ref
  1.6 0.0 copy-start
  1.6 1.6 %copy-done = s32[2048,256]{1,0:T(8,128)S(1)} copy-done((s32[2048,256]{1,0:T(8,128)S(1)}, s32[2048,256]{1,0:T(8,128)}, u32[]{:S(2)}) %copy-start) | copy-done | bytes 2097176
  3.2 124.9 %shard_map.37 = bf16[32,256,2,256]{3,2,1,0:T(2,128)(2,1)S(1)} custom-call(s32[2048,256]{1,0:T(8,128)S(1)} %copy-done, bf16[208,256]{1,0:T(8,128)(2,1)S(1)} %fusion.1.table_ref), custom_call_target="tpu_custom_call" | custom-call | tf_op jit(solution)/shard_map/pallas_call | solution.py:364
  128.1 3.4 %copy.5 = bf16[32,256,2,256]{3,2,1,0:T(2,128)(2,1)} copy(bf16[32,256,2,256]{3,2,1,0:T(2,128)(2,1)S(1)} %shard_map.37) | data formatting | bytes 16777216
Async XLA Ops:
  1.6 1.6 %copy-start = (s32[2048,256]{1,0:T(8,128)S(1)}, s32[2048,256]{1,0:T(8,128)}, u32[]{:S(2)}) copy-start(s32[2048,256]{1,0:T(8,128)} %raw_ref.1) | copy-start | bytes 6291460

commit v3 on v2

--- a/solution.py
+++ b/solution.py
@@ -20,8 +20,10 @@
 SPLIT = 2
 GROUP = 2
 GROUPS = UNITS // GROUP
-LEAD = 4
+LEAD = 6
 END = 8 * LAG // 2
+TAIL = UNITS - 6
+TAIL_END = 5 * LAG // 2 + 4
 RIM = TAPS - 1
 STRIPS = [(11, 15), (7, 11), (3, 7), (0, 3)]
 MESH = pl.DeviceIdType.MESH
@@ -161,6 +163,13 @@
     back = (8 - dz) % 8 + jnp.where(main, 0, 1)
     begin = [LAG * hops // 2, LAG * back // 2]
     more = [dz != 7, dz != 1]
+    source = dz == 0
+    tail_hops = jnp.minimum(dz, (8 - dz) % 8) + jnp.where(main, 0, 1)
+    tail_begin = LAG * tail_hops // 2
+    tail_more = [
+        jnp.logical_or(source, jnp.logical_and(dz >= 1, dz <= 3)),
+        jnp.logical_or(source, dz >= 6),
+    ]
 
     def remote(src, dst, send, recv, peer):
         return pltpu.make_async_remote_copy(
@@ -249,7 +258,7 @@
         for h in range(2):
             u = t - begin[h]
 
-            @pl.when(jnp.logical_and(u >= 0, u < UNITS))
+            @pl.when(jnp.logical_and(u >= 0, u < TAIL))
             def _():
                 @pl.when(root)
                 def _():
@@ -286,6 +295,48 @@
                             z_next[h],
                         ).start()
 
+        w = t - tail_begin
+
+        @pl.when(jnp.logical_and(w >= TAIL, w < UNITS))
+        def _():
+            for h in range(2):
+                @pl.when(root)
+                def _():
+                    for d in range(2):
+                        remote(
+                            a.at[w, h], b.at[w, h], out_sem.at[12 + d], z_sem.at[h, w], z_next[d]
+                        ).start()
+                    remote(
+                        a.at[w, h, rest], b.at[w, h, rest], out_sem.at[7 + h], z_sem.at[h, w], pair
+                    ).start()
+                    pltpu.make_async_copy(a.at[w, h], b.at[w, h], f_sem.at[h, w]).start()
+
+                @pl.when(jnp.logical_and(main, jnp.logical_not(root)))
+                def _():
+                    arrived(b.at[w, h], z_sem.at[h, w])
+                    for d in range(2):
+                        @pl.when(tail_more[d])
+                        def _():
+                            remote(
+                                b.at[w, h], b.at[w, h], out_sem.at[12 + d], z_sem.at[h, w],
+                                z_next[d],
+                            ).start()
+
+                    remote(
+                        b.at[w, h, far], b.at[w, h, far], out_sem.at[7 + h], f_sem.at[h, w], pair
+                    ).start()
+
+                @pl.when(jnp.logical_not(main))
+                def _():
+                    arrived(b.at[w, h, rest], z_sem.at[h, w])
+                    for d in range(2):
+                        @pl.when(tail_more[d])
+                        def _():
+                            remote(
+                                b.at[w, h, rest], b.at[w, h, rest], out_sem.at[12 + d],
+                                z_sem.at[h, w], z_next[d],
+                            ).start()
+
         @pl.when(jnp.logical_and(helper, jnp.logical_and(t >= 0, t < UNITS)))
         def _():
             for h in range(2):
@@ -293,9 +344,17 @@
                     a.at[t, h, far], b.at[t, h, far], out_sem.at[9 + h], f_sem.at[h, t], cross
                 ).start()
 
-        v = t - END - 1
-
-        @pl.when(jnp.logical_and(v >= 0, v % 2 == 0))
+        first = t - END - 1
+        last = t - TAIL_END
+        ends = last % 2 == 0
+        v = jnp.where(ends, last, first)
+
+        @pl.when(
+            jnp.logical_or(
+                jnp.logical_and(ends, jnp.logical_and(last >= TAIL, last < UNITS)),
+                jnp.logical_and(jnp.logical_not(ends), jnp.logical_and(first >= 0, first < TAIL)),
+            )
+        )
         def _():
             for e in range(2):
                 for h in range(2):
@@ -321,7 +380,7 @@
 
         return carry
 
-    lax.fori_loop(0, UNITS + END + 2 * LEAD, step, 0)
+    lax.fori_loop(0, max(TAIL + END, UNITS + TAIL_END) + 2 * LEAD, step, 0)
 
     def left(src, sem):
         remote(src, src, sem, sem, pair).wait_send()
@@ -337,11 +396,19 @@
     for h in range(2):
         @pl.when(jnp.logical_and(main, more[h]))
         def _():
-            left(b.at[:, h], out_sem.at[5 + h])
+            left(b.at[pl.ds(0, TAIL), h], out_sem.at[5 + h])
+
+        @pl.when(jnp.logical_and(main, tail_more[h]))
+        def _():
+            left(b.at[pl.ds(TAIL, UNITS - TAIL)], out_sem.at[12 + h])
+
+        @pl.when(jnp.logical_and(jnp.logical_not(main), tail_more[h]))
+        def _():
+            left(b.at[pl.ds(TAIL, UNITS - TAIL), :, rest], out_sem.at[12 + h])
 
         @pl.when(jnp.logical_and(jnp.logical_not(main), more[h]))
         def _():
-            left(b.at[:, h, rest], out_sem.at[5 + h])
+            left(b.at[pl.ds(0, TAIL), h, rest], out_sem.at[5 + h])
 
         @pl.when(root)
         def _():
@@ -380,7 +447,7 @@
             dma((GROUPS,)),
             dma((2, UNITS)),
             dma((2, UNITS)),
-            dma((12,)),
+            dma((14,)),
         ],
         compiler_params=pltpu.CompilerParams(
             collective_id=0, has_side_effects=True, vmem_limit_bytes=30 * 1024 * 1024

time: 132 us -> 129 us (0.977)
  Pallas kernels: 125 us -> 122 us
    pallas_call x1, Pallas kernels: 125 us -> 122 us  [body(): pl.pallas_call(gather_correlate, out_shape=jax.ShapeDtypeStruct((CHANNELS...]
where the time goes in v3:
time: 129 us; the launch traced here: 128 us
  Pallas kernels  122 us (95%)
  local copies, waits for them, and re-layouts  4.99 us (4%)
  other arithmetic  1.6 us (1%)
    pallas_call x1, Pallas kernels, body(): pl.pallas_call(gather_correlate, out_shape=jax.ShapeDtypeStruct((CHANNELS...  122 us
    unnamed x3, local copies, waits for them, and re-layouts  4.99 us

profile of v3, /device:TPU:24, one launch (start us, length us, event | category | flops | bytes accessed | tf_op | source)
XLA Modules:
  0.0 128.3 jit_solution(11315488436313718524)
XLA Ops:
  0.0 0.7 convert.4
  0.7 0.9 fusion.1.table_ref
  1.6 0.0 copy-start
  1.6 1.6 %copy-done = s32[2048,256]{1,0:T(8,128)S(1)} copy-done((s32[2048,256]{1,0:T(8,128)S(1)}, s32[2048,256]{1,0:T(8,128)}, u32[]{:S(2)}) %copy-start) | copy-done | bytes 2097176
  3.2 121.7 %shard_map.37 = bf16[32,256,2,256]{3,2,1,0:T(2,128)(2,1)S(1)} custom-call(s32[2048,256]{1,0:T(8,128)S(1)} %copy-done, bf16[208,256]{1,0:T(8,128)(2,1)S(1)} %fusion.1.table_ref), custom_call_target="tpu_custom_call" | custom-call | tf_op jit(solution)/shard_map/pallas_call | solution.py:431
  124.9 3.4 %copy.5 = bf16[32,256,2,256]{3,2,1,0:T(2,128)(2,1)} copy(bf16[32,256,2,256]{3,2,1,0:T(2,128)(2,1)S(1)} %shard_map.37) | data formatting | bytes 16777216
Async XLA Ops:
  1.6 1.6 %copy-start = (s32[2048,256]{1,0:T(8,128)S(1)}, s32[2048,256]{1,0:T(8,128)}, u32[]{:S(2)}) copy-start(s32[2048,256]{1,0:T(8,128)} %raw_ref.1) | copy-start | bytes 6291460

commit v4 on v3

--- a/solution.py
+++ b/solution.py
@@ -2,8 +2,6 @@
 
 import jax
 import jax.numpy as jnp
-import ml_dtypes
-import numpy as np
 from jax import lax
 from jax.experimental import pallas as pl
 from jax.experimental.pallas import tpu as pltpu
@@ -29,21 +27,23 @@
 MESH = pl.DeviceIdType.MESH
 
 
-def dft_tables():
-    sample = np.arange(TRANSFORM)[None, :]
-    channel = np.arange(1, CHANNELS + 1)[:, None]
-    phase = (sample * channel % TRANSFORM) * (2.0 * math.pi / TRANSFORM)
-    rest = np.stack([np.cos(phase), -np.sin(phase)], axis=1).reshape(UNITS, TRANSFORM)
-    rest = rest.astype(np.float32)
+def dft_table(table_ref):
+    row = lax.broadcasted_iota(jnp.int32, (UNITS, TRANSFORM), 0)
+    sample = lax.broadcasted_iota(jnp.int32, (UNITS, TRANSFORM), 1)
+    turn = (sample * ((row >> 1) + 1) + (TRANSFORM // 4) * (row & 1)) & (TRANSFORM - 1)
+    turn = jnp.minimum(turn, TRANSFORM - turn)
+    rest = jnp.cos(turn.astype(jnp.float32) * (2.0 * math.pi / TRANSFORM))
     parts = []
     for _ in range(3):
-        part = rest.astype(ml_dtypes.bfloat16)
-        rest = rest - part.astype(np.float32)
+        part = rest.astype(jnp.bfloat16)
+        rest = rest - part.astype(jnp.float32)
         parts.append(part)
     one, two, three = parts
-    first = np.block([[one, one], [three, two]])
-    second = np.block([[two, one]])
-    return np.concatenate([first, second], axis=0)
+    for i, pair in enumerate(((one, one), (three, two), (two, one))):
+        for half in range(2):
+            table_ref[i * UNITS : (i + 1) * UNITS, half * TRANSFORM : (half + 1) * TRANSFORM] = (
+                pair[half]
+            )
 
 
 def product(a, b):
@@ -89,8 +89,8 @@
     lax.fori_loop(0, TRANSFORM // 16, tile, 0)
 
 
-def spread_taps(table_ref, spread):
-    taps = table_ref[3 * UNITS :, :TRANSFORM]
+def spread_taps(taps_in, spread):
+    taps = taps_in[...].astype(jnp.float32).astype(jnp.bfloat16)
     index = lax.broadcasted_iota(jnp.int32, (TAPS, 128), 0)
     for p in range(TAPS):
         pick = jnp.where(index == p, 1.0, 0.0).astype(jnp.bfloat16)
@@ -124,8 +124,8 @@
 
 
 def gather_correlate(
-    raw_ref, table_ref, o_ref, a, b, rim, own_rim, acc, flat, taps_ref, rim_sem, y_sem, x_sem,
-    s_sem, z_sem, f_sem, out_sem,
+    raw_ref, taps_in, o_ref, a, b, rim, own_rim, acc, flat, taps_ref, table_ref, rim_sem, y_sem,
+    x_sem, s_sem, z_sem, f_sem, out_sem,
 ):
     r = lax.axis_index("row")
     c = lax.axis_index("col")
@@ -150,7 +150,8 @@
     before = (r, (c + 15) % 16)
     for peer in z_next + x_next + [pair, cross, sibling, across, after, before]:
         pl.semaphore_signal(barrier, inc=1, device_id=peer, device_id_type=MESH)
-    spread_taps(table_ref, taps_ref)
+    dft_table(table_ref)
+    spread_taps(taps_in, taps_ref)
     for s in range(RIM):
         own_rim[s] = raw_ref[(s + 1) * TRANSFORM : (s + 2) * TRANSFORM, :].astype(jnp.bfloat16)
     pl.semaphore_wait(barrier, 11)
@@ -224,36 +225,9 @@
     def step(i, carry):
         t = i - 2 * LEAD
 
-        @pl.when(jnp.logical_and(t % GROUP == 0, t < UNITS))
-        def _():
-            j = t // GROUP
-
-            @pl.when(t >= 0)
-            def _():
-                arrived(a.at[pl.ds(j * GROUP, GROUP), 1 - co], s_sem.at[j])
-
-            m = j + 2 * LEAD // GROUP
-
-            @pl.when(m < GROUPS)
-            def _():
-                rows = pl.ds(m * GROUP, GROUP)
-                arrived(a.at[rows, co, at_x + 1 - yh], y_sem.at[m])
-                for d in range(3):
-                    remote(
-                        a.at[rows, co, pl.ds(at_x, 2)], a.at[rows, co, pl.ds(at_x, 2)], out_sem.at[1 + d],
-                        x_sem.at[d, m], x_next[d],
-                    ).start()
-
-            n = j + LEAD // GROUP
-
-            @pl.when(jnp.logical_and(n >= 0, n < GROUPS))
-            def _():
-                rows = pl.ds(n * GROUP, GROUP)
-                for d in range(3):
-                    arrived(a.at[rows, co, pl.ds((x + 3 - d) % 4 * 2, 2)], x_sem.at[d, n])
-                remote(
-                    a.at[rows, co], a.at[rows, co], out_sem.at[4], s_sem.at[n], sibling
-                ).start()
+        @pl.when(jnp.logical_and(t % GROUP == 0, jnp.logical_and(t >= 0, t < UNITS)))
+        def _():
+            arrived(a.at[pl.ds(t, GROUP), 1 - co], s_sem.at[t // GROUP])
 
         for h in range(2):
             u = t - begin[h]
@@ -342,6 +316,33 @@
             for h in range(2):
                 remote(
                     a.at[t, h, far], b.at[t, h, far], out_sem.at[9 + h], f_sem.at[h, t], cross
+                ).start()
+
+        @pl.when(jnp.logical_and(t % GROUP == 0, t < UNITS))
+        def _():
+            j = t // GROUP
+
+            m = j + 2 * LEAD // GROUP
+
+            @pl.when(m < GROUPS)
+            def _():
+                rows = pl.ds(m * GROUP, GROUP)
+                arrived(a.at[rows, co, at_x + 1 - yh], y_sem.at[m])
+                for d in range(3):
+                    remote(
+                        a.at[rows, co, pl.ds(at_x, 2)], a.at[rows, co, pl.ds(at_x, 2)], out_sem.at[1 + d],
+                        x_sem.at[d, m], x_next[d],
+                    ).start()
+
+            n = j + LEAD // GROUP
+
+            @pl.when(jnp.logical_and(n >= 0, n < GROUPS))
+            def _():
+                rows = pl.ds(n * GROUP, GROUP)
+                for d in range(3):
+                    arrived(a.at[rows, co, pl.ds((x + 3 - d) % 4 * 2, 2)], x_sem.at[d, n])
+                remote(
+                    a.at[rows, co], a.at[rows, co], out_sem.at[4], s_sem.at[n], sibling
                 ).start()
 
         first = t - END - 1
@@ -424,8 +425,6 @@
 
 
 def body(raw, taps):
-    wide = jnp.concatenate([taps, jnp.zeros_like(taps)], axis=1).astype(jnp.bfloat16)
-    table = jnp.concatenate([dft_tables(), wide], axis=0)
     block = (UNITS, 2, 8, SPECTRA_DEV, SIDE)
     dma = pltpu.SemaphoreType.DMA
     return pl.pallas_call(
@@ -441,6 +440,7 @@
             pltpu.VMEM((SPECTRA_DEV, TRANSFORM, SIDE), jnp.float32),
             pltpu.VMEM((2, SPECTRA_DEV * UNITS, 128), jnp.float32),
             pltpu.VMEM((TAPS, TRANSFORM, 128), jnp.float32),
+            pltpu.VMEM((3 * UNITS, SIDE), jnp.bfloat16),
             dma((len(STRIPS),)),
             dma((GROUPS,)),
             dma((3, GROUPS)),
@@ -452,7 +452,7 @@
         compiler_params=pltpu.CompilerParams(
             collective_id=0, has_side_effects=True, vmem_limit_bytes=30 * 1024 * 1024
         ),
-    )(raw, table)
+    )(raw, taps)
 
 
 def solution(mesh):

time: 129 us -> 127 us (0.984)
  Pallas kernels: 122 us -> 120 us
  other arithmetic: 1.6 us -> 0 us
    unnamed x3 -> x5, local copies, waits for them, and re-layouts: 4.99 us -> 5.69 us
where the time goes in v4:
time: 127 us; the launch traced here: 126 us
  Pallas kernels  120 us (94%)
  local copies, waits for them, and re-layouts  5.69 us (4%)
    pallas_call x1, Pallas kernels, body(): pl.pallas_call(gather_correlate, out_shape=jax.ShapeDtypeStruct((CHANNELS...  120 us
    unnamed x5, local copies, waits for them, and re-layouts  5.69 us

profile of v4, /device:TPU:24, one launch (start us, length us, event | category | flops | bytes accessed | tf_op | source)
XLA Modules:
  0.0 126.1 jit_solution(11977300564963234361)
XLA Ops:
  0.0 0.0 copy-start
  0.0 1.6 %copy-done = s32[2048,256]{1,0:T(8,128)S(1)} copy-done((s32[2048,256]{1,0:T(8,128)S(1)}, s32[2048,256]{1,0:T(8,128)}, u32[]{:S(2)}) %copy-start) | copy-done | bytes 2097176
  1.6 0.0 copy-start.1
  1.6 0.7 copy-done.1
  2.3 120.4 %shard_map.28 = bf16[32,256,2,256]{3,2,1,0:T(2,128)(2,1)S(1)} custom-call(s32[2048,256]{1,0:T(8,128)S(1)} %copy-done, s32[16,128]{1,0:T(8,128)S(1)} %copy-done.1), custom_call_target="tpu_custom_call" | custom-call | tf_op jit(solution)/shard_map/pallas_call | solution.py:430
  122.7 3.4 %copy.4 = bf16[32,256,2,256]{3,2,1,0:T(2,128)(2,1)} copy(bf16[32,256,2,256]{3,2,1,0:T(2,128)(2,1)S(1)} %shard_map.28) | data formatting | bytes 16777216
Async XLA Ops:
  0.0 1.6 %copy-start = (s32[2048,256]{1,0:T(8,128)S(1)}, s32[2048,256]{1,0:T(8,128)}, u32[]{:S(2)}) copy-start(s32[2048,256]{1,0:T(8,128)} %raw_ref.1) | copy-start | bytes 6291460
  1.6 0.7 copy-start.1

commit v5 on v4

--- a/solution.py
+++ b/solution.py
@@ -14,16 +14,16 @@
 SPECTRA = 256
 UNITS = 2 * CHANNELS
 SIDE = 256
-LAG = 8
+LAG = 9
 SPLIT = 2
 GROUP = 2
 GROUPS = UNITS // GROUP
 LEAD = 6
-END = 8 * LAG // 2
+END = 36
 TAIL = UNITS - 6
-TAIL_END = 5 * LAG // 2 + 4
+TAIL_END = 26
 RIM = TAPS - 1
-STRIPS = [(11, 15), (7, 11), (3, 7), (0, 3)]
+STRIPS = [(8, 15), (3, 8), (0, 3)]
 MESH = pl.DeviceIdType.MESH
 
 

time: 127 us -> 128 us (level)
  no operation moved by 1% of the time
where the time goes in v5:
time: 128 us; the launch traced here: 126 us
  Pallas kernels  120 us (94%)
  local copies, waits for them, and re-layouts  5.69 us (4%)
    pallas_call x1, Pallas kernels, body(): pl.pallas_call(gather_correlate, out_shape=jax.ShapeDtypeStruct((CHANNELS...  120 us
    unnamed x5, local copies, waits for them, and re-layouts  5.69 us

profile of v5, /device:TPU:24, one launch (start us, length us, event | category | flops | bytes accessed | tf_op | source)
XLA Modules:
  0.0 126.0 jit_solution(1703703349718086923)
XLA Ops:
  0.0 0.0 copy-start
  0.0 1.6 %copy-done = s32[2048,256]{1,0:T(8,128)S(1)} copy-done((s32[2048,256]{1,0:T(8,128)S(1)}, s32[2048,256]{1,0:T(8,128)}, u32[]{:S(2)}) %copy-start) | copy-done | bytes 2097176
  1.6 0.0 copy-start.1
  1.6 0.7 copy-done.1
  2.3 120.3 %shard_map.28 = bf16[32,256,2,256]{3,2,1,0:T(2,128)(2,1)S(1)} custom-call(s32[2048,256]{1,0:T(8,128)S(1)} %copy-done, s32[16,128]{1,0:T(8,128)S(1)} %copy-done.1), custom_call_target="tpu_custom_call" | custom-call | tf_op jit(solution)/shard_map/pallas_call | solution.py:430
  122.6 3.4 %copy.4 = bf16[32,256,2,256]{3,2,1,0:T(2,128)(2,1)} copy(bf16[32,256,2,256]{3,2,1,0:T(2,128)(2,1)S(1)} %shard_map.28) | data formatting | bytes 16777216
Async XLA Ops:
  0.0 1.6 %copy-start = (s32[2048,256]{1,0:T(8,128)S(1)}, s32[2048,256]{1,0:T(8,128)}, u32[]{:S(2)}) copy-start(s32[2048,256]{1,0:T(8,128)} %raw_ref.1) | copy-start | bytes 6291460
  1.6 0.7 copy-start.1
